TPU v7x, 1024 devices: a whole 4x8x16 slice. The times are simulated.
1024 devices in a mesh: ri: 8 (over x, core), row: 8 (over y), col: 16 (over z).
Axes of the slice: x: 4, y: 8, z: 16, core: 2. Of those that a mesh axis runs over, the one named last changes fastest.
Arguments:
- three_centre: bfloat16 [64, 1024, 8192], P('ri', 'row', 'col'), may hold values from -0.5 to 0.5
- density_band: bfloat16 [8192, 5, 128], P('col'), may hold values from -0.25 to 0.25
- band_mask: int32 [64, 5], P('col'), may hold values 0 or 1
Outputs:
- exchange: float32 [1024, 1024], P('col', 'row')
All inputs are finite; a program needn't handle non-finite values. No bound on the sum of `band_mask` on one device may be relied on, other than what follows from the above.
Results may differ from a plain program's by a relative error of at most 0.0029.
Values may be sent and summed in bfloat16 or wider, within the bound.
A program may use at most 32 MiB of HBM per device.

v0:
```python
import jax
import jax.numpy as jnp
from jax import lax
from jax.sharding import PartitionSpec as P


def from_behind(shard, axis, by):
    length = lax.axis_size(axis)
    return lax.ppermute(shard, axis, [(i, (i + by) % length) for i in range(length)])


def per_device(three_centre, density_band, band_mask):
    band_count = density_band.shape[1]
    centre = band_count // 2
    col_orb = density_band.shape[2]
    blocks = band_mask.shape[0]
    funcs = three_centre.shape[0]
    rows = three_centre.shape[1]
    weights = jnp.repeat(band_mask.astype(jnp.float32), col_orb, axis=0)
    density = (density_band.astype(jnp.float32) * weights[:, :, None]).astype(jnp.bfloat16)
    tensor_blocks = three_centre.reshape(funcs, rows, blocks, col_orb)
    density_blocks = density.reshape(blocks, col_orb, band_count, col_orb)
    extended = jnp.zeros((funcs, rows, blocks + 2 * centre, col_orb), jnp.float32)
    for column in range(band_count):
        part = jnp.einsum(
            "pmbl,bls->pmbs",
            tensor_blocks,
            density_blocks[:, :, column, :],
            preferred_element_type=jnp.float32,
        )
        extended = extended.at[:, :, column : column + blocks].add(part)
    upper_rim = extended[:, :, blocks + centre :]
    lower_rim = extended[:, :, :centre]
    from_lower = from_behind(upper_rim, "col", 1)
    from_upper = from_behind(lower_rim, "col", -1)
    mixed = extended[:, :, centre : centre + blocks]
    mixed = mixed.at[:, :, :centre].add(from_lower)
    mixed = mixed.at[:, :, blocks - centre :].add(from_upper)
    mixed_low = mixed.reshape(funcs, rows, blocks * col_orb).astype(jnp.bfloat16)
    terms = jnp.einsum(
        "pns,pms->nm",
        lax.all_gather(three_centre, "row", axis=1, tiled=True),
        mixed_low,
        preferred_element_type=jnp.float32,
    )
    summed = lax.psum_scatter(terms, "col", scatter_dimension=0, tiled=True)
    return lax.psum(summed, "ri")


def solution(mesh):
    placed = (P("ri", "row", "col"), P("col", None, None), P("col", None))
    return jax.shard_map(
        per_device, mesh=mesh, in_specs=placed, out_specs=P("col", "row"), check_vma=False
    )
```

profile of v0, /device:TPU:1, one launch (start us, length us, event | category | flops | bytes accessed | tf_op | source)
XLA Modules:
  0.0 231.1 jit_solution(6894418151261791791)
XLA Ops:
  6.5 0.0 all-gather.2.cloned.1.call-start
  6.5 0.7 all-gather.2.cloned.1.call-update
  7.3 0.0 reduce-scatter.4.cloned.1.call-start
  7.3 0.7 convert_element_type.16
  8.0 0.1 copy.25
  8.1 0.1 broadcast_bitcast_fusion
  8.2 1.5 multiply_convert_fusion
  9.7 0.0 copy-done
  9.7 0.5 convolution_bitcast_fusion
  10.2 0.5 scatter-add.24
  10.7 0.8 fusion.2
  11.5 0.8 fusion.1
  12.3 0.8 fusion
  13.2 1.0 constant_dynamic-update-slice_fusion
  14.2 0.1 slice.250
  14.2 4.8 %collective-permute-start = (f32[8,128,2,128]{1,3,0,2:T(8,128)S(1)}, f32[8,128,2,128]{1,3,0,2:T(8,128)S(1)}, u32[]{:S(2)}, u32[]{:S(2)}) collective-permute-start(f32[8,128,2,128]{1,3,0,2:T(8,128)S(1)} %slice.250), channel_id=1, source_target_pairs={{0,1},{1,2},{2,3},{3,4},{4,5},{5,6},{6,7},{7,8},{8,9},{9,10},{10,1... | collective-permute-start | bytes 3145736 | tf_op jit(solution)/shard_map/ppermute | solution.py:9
  19.1 0.2 slice.248
  19.3 36.7 %collective-permute-done = f32[8,128,2,128]{1,3,0,2:T(8,128)S(1)} collective-permute-done((f32[8,128,2,128]{1,3,0,2:T(8,128)S(1)}, f32[8,128,2,128]{1,3,0,2:T(8,128)S(1)}, u32[]{:S(2)}, u32[]{:S(2)}) %collective-permute-start) | collective-permute-done | bytes 1048608 | tf_op jit(solution)/shard_map/ppermute | solution.py:9
  56.0 0.2 fusion.15
  56.2 3.1 %collective-permute-start.1 = (f32[8,128,2,128]{1,3,0,2:T(8,128)S(1)}, f32[8,128,2,128]{1,3,0,2:T(8,128)S(1)}, u32[]{:S(2)}, u32[]{:S(2)}) collective-permute-start(f32[8,128,2,128]{1,3,0,2:T(8,128)S(1)} %get-tuple-element.89), channel_id=1, source_target_pairs={{0,15},{1,0},{2,1},{3,2},{4,3},{5,4},{6,5},{7,6},{8,7},{9,8},{10,9... | collective-permute-start | bytes 3145736 | tf_op jit(solution)/shard_map/ppermute | solution.py:9
  59.3 22.5 %collective-permute-done.1 = f32[8,128,2,128]{1,3,0,2:T(8,128)S(1)} collective-permute-done((f32[8,128,2,128]{1,3,0,2:T(8,128)S(1)}, f32[8,128,2,128]{1,3,0,2:T(8,128)S(1)}, u32[]{:S(2)}, u32[]{:S(2)}) %collective-permute-start.1) | collective-permute-done | bytes 1048608 | tf_op jit(solution)/shard_map/ppermute | solution.py:9
  81.8 0.3 fusion.8
  82.0 0.2 convert_element_type.18
  82.2 0.1 copy.36
  82.3 37.9 %all-gather.2.cloned.1.call-done = bf16[8,1024,512]{2,1,0:T(8,128)(2,1)} async-done(((bf16[8,128,512]{2,1,0:T(8,128)(2,1)}), bf16[8,1024,512]{2,1,0:T(8,128)(2,1)}) %all-gather.2.cloned.1.call-update) | async-done | bytes 8388624 | tf_op jit(solution)/shard_map/all_gather | solution.py:42
  120.2 6.3 %convolution_bitcast_fusion.1 = f32[1024,128]{0,1:T(8,128)S(1)} fusion(bf16[8,128,512]{1,2,0:T(8,128)(2,1)S(1)} %bitcast.94, bf16[8,1024,512]{2,1,0:T(8,128)(2,1)} %all-gather.2.cloned.1.call-done), kind=kOutput, calls=%fused_computation.9 | convolution fusion | flops 1073741824 | bytes 9961472 | tf_op jit(solution)/shard_map/pns,pms->nm/dot_general | solution.py:40
  126.4 1.0 copy.45
  127.4 0.0 reduce-scatter.4.cloned.1.call-update
  127.5 62.3 %reduce-scatter.4.cloned.1.call-done = f32[64,128]{1,0:T(8,128)} async-done(((f32[1024,128]{1,0:T(8,128)}), f32[64,128]{1,0:T(8,128)}) %reduce-scatter.4.cloned.1.call-update) | async-done | bytes 32784
  189.8 0.8 copy.46
  190.7 32.9 %psum.7 = f32[64,128]{0,1:T(8,128)S(1)} all-reduce(f32[64,128]{0,1:T(8,128)S(1)} %copy.46), channel_id=1, replica_groups=mesh['ri'=8,'row'=8,'col'=16] {'ri'}, use_global_device_ids=true, to_apply=%region_1.0 | all-reduce | flops 8192 | bytes 65536 | tf_op jit(solution)/shard_map/psum | solution.py:47
  223.5 0.7 copy.38
  (2 shorter events, 0.0 us)
Async XLA Ops:
  6.5 3.1 %copy-start = (bf16[8,128,512]{2,1,0:T(8,128)(2,1)S(1)}, bf16[8,128,512]{2,1,0:T(8,128)(2,1)}, u32[]{:S(2)}) copy-start(bf16[8,128,512]{2,1,0:T(8,128)(2,1)} %param.17) | copy-start | bytes 3145732
  6.5 113.6 %all-gather.2.cloned.1.call-start = ((), (), s32[]{:S(2)}) async-start(), calls=%async_computation.1 | async-start | bytes 9437184 | tf_op jit(solution)/shard_map/all_gather | solution.py:42
  7.3 182.5 %reduce-scatter.4.cloned.1.call-start = ((), (), s32[]{:S(2)}) async-start(), calls=%async_computation.2 | async-start | bytes 557056
  14.2 41.7 %collective-permute-start = (f32[8,128,2,128]{1,3,0,2:T(8,128)S(1)}, f32[8,128,2,128]{1,3,0,2:T(8,128)S(1)}, u32[]{:S(2)}, u32[]{:S(2)}) collective-permute-start(f32[8,128,2,128]{1,3,0,2:T(8,128)S(1)} %slice.250), channel_id=1, source_target_pairs={{0,1},{1,2},{2,3},{3,4},{4,5},{5,6},{6,7},{7,8},{8,9},{9,10},{10,1... | collective-permute-start | bytes 3145736 | tf_op jit(solution)/shard_map/ppermute | solution.py:9
  56.2 25.6 %collective-permute-start.1 = (f32[8,128,2,128]{1,3,0,2:T(8,128)S(1)}, f32[8,128,2,128]{1,3,0,2:T(8,128)S(1)}, u32[]{:S(2)}, u32[]{:S(2)}) collective-permute-start(f32[8,128,2,128]{1,3,0,2:T(8,128)S(1)} %get-tuple-element.89), channel_id=1, source_target_pairs={{0,15},{1,0},{2,1},{3,2},{4,3},{5,4},{6,5},{7,6},{8,7},{9,8},{10,9... | collective-permute-start | bytes 3145736 | tf_op jit(solution)/shard_map/ppermute | solution.py:9
Sparse Core Ops, SparseCore 0:
  10.0 110.1 all-gather.1
  127.6 62.1 reduce-scatter.3
where the time goes:
time: 233 us; the launch traced here: 231 us
  waiting for transfers between devices  160 us (69%)
  blocking collectives  32.9 us (14%)
  between operations  13.5 us (6%)
  matrix products  10.2 us (4%)
  starting transfers between devices  7.94 us (3%)
  local copies, waits for them, and re-layouts  3.6 us (2%)
  other arithmetic  2.81 us (1%)
    unnamed x3, waiting for transfers between devices  63.1 us
    ppermute x2, waiting for transfers between devices, from_behind(): lax.ppermute(shard, axis, [(i, (i + by) % length) for i in range(length)])  59.2 us
    all_gather x1, waiting for transfers between devices, per_device(): lax.all_gather(three_centre, 'row', axis=1, tiled=True)  37.9 us
    psum x1, blocking collectives, per_device(): return lax.psum(summed, 'ri')  32.9 us
    ppermute x2, starting transfers between devices, from_behind(): lax.ppermute(shard, axis, [(i, (i + by) % length) for i in range(length)])  7.9 us
    dot_general x1, matrix products, per_device(): jnp.einsum('pns,pms->nm', lax.all_gather(three_centre, 'row', axis=1, til...  6.25 us
  transfers between devices with their start and end apart: 4, of which 4 were waited for; matrix products, arithmetic and copies ran while one was open for 3% of the time, Pallas kernels for 0%

commit v1 on v0

v1 whole, which is shorter than its diff:
```python
import jax
import jax.numpy as jnp
from jax import lax
from jax.experimental import pallas as pl
from jax.experimental.pallas import tpu as pltpu
from jax.sharding import PartitionSpec as P

CORES = 2
BF16 = jnp.bfloat16
F32 = jnp.float32


def arrival_order(length):
    order = [0]
    for step in range(1, length // 2 + 1):
        for offset in (step, (length - step) % length):
            if offset not in order:
                order.append(offset)
    return order


def make_kernel(nx, ny, nz, col_orb, blocks, band):
    centre = band // 2
    rim = centre * col_orb
    length = blocks * col_orb
    half = ny // CORES

    def kernel(
        tensor, density, mask, out,
        ext, dens, dens_low, dens_high, big, mixed,
        x_own, x_send, x_recv, z_send, z_recv, z_sum, y_send, y_recv, gathered,
        own_sem, a_send, a_recv, c_send, c_recv, hl_send, hl_recv, hr_send, hr_recv,
        d_sem, dl_send, dl_recv, dh_send, dh_recv,
        xs_sem, xr_sem, zs_sem, zr_sem, ys_sem, yr_sem, bs_sem, br_sem,
    ):
        ri = lax.axis_index("ri")
        y = lax.axis_index("row")
        z = lax.axis_index("col")
        x = ri // CORES
        core = lax.rem(ri, CORES)
        per_block = tensor.shape[1]
        owner = y // half

        def place(to_x=x, to_core=core, to_y=y, to_z=z):
            return {"ri": to_x * CORES + to_core, "row": to_y, "col": to_z}

        def send(source, target, send_sem, recv_sem, device):
            return pltpu.make_async_remote_copy(
                src_ref=source, dst_ref=target, send_sem=send_sem, recv_sem=recv_sem,
                device_id=device, device_id_type=pl.DeviceIdType.MESH,
            )

        z_up = lax.rem(z + 1, nz)
        z_down = lax.rem(z + nz - 1, nz)

        barrier = pltpu.get_barrier_semaphore()
        partners = [place(to_y=lax.rem(y + k, ny)) for k in range(1, ny)]
        partners += [place(to_z=lax.rem(z + k, nz)) for k in range(1, nz)]
        partners += [place(to_core=1 - core, to_z=z_up), place(to_core=1 - core, to_z=z_down)]
        partners += [place(to_core=1 - core)]
        for k in range(1, nx):
            for flip in (core, 1 - core):
                partners.append(place(to_x=lax.rem(x + k, nx), to_core=flip))
        for partner in partners:
            pl.semaphore_signal(barrier, inc=1, device_id=partner, device_id_type=pl.DeviceIdType.MESH)

        load = pltpu.make_async_copy(density, dens, d_sem)
        load.start()
        mine = pl.ds(y * per_block, per_block)
        middle = pl.ds(rim, length)
        own = pltpu.make_async_copy(tensor.at[y], ext.at[core, mine, :, :, middle], own_sem)
        own.start()
        big[...] = jnp.zeros_like(big)
        load.wait()
        for b in range(blocks):
            for c in range(band):
                weight = mask[b, c].astype(F32)
                rows = slice(b * col_orb, (b + 1) * col_orb)
                dens[c, rows, :] = (dens[c, rows, :].astype(F32) * weight).astype(BF16)
        pl.semaphore_wait(barrier, len(partners))

        started = []
        order = arrival_order(ny)
        for k in order[1:]:
            to = lax.rem(y + k, ny)
            copy = send(tensor.at[to], ext.at[core, mine, :, :, middle], a_send.at[k - 1], a_recv.at[k - 1], place(to_y=to))
            copy.start()
            started.append(copy)
        d_up = send(dens.at[pl.ds(centre + 1, centre), pl.ds(length - rim, rim)], dens_low, dl_send, dl_recv, place(to_z=z_up))
        d_down = send(dens.at[pl.ds(0, centre), pl.ds(0, rim)], dens_high, dh_send, dh_recv, place(to_z=z_down))
        d_up.start()
        d_down.start()

        def part(e, t):
            return slice((e % 2 + 2 * ((e - 2 * (t // 2)) // 2)) * col_orb, (e % 2 + 2 * ((e - 2 * (t // 2)) // 2) + 1) * col_orb), slice((t % 2) * col_orb, (t % 2 + 1) * col_orb)

        for t in range(blocks):
            for e in range(max(t, centre), min(t + band, centre + blocks)):
                rows, cols = part(e, t)
                local = e - centre
                big[t // 2, rows, cols] = dens[band - 1 - (e - t), local * col_orb : (local + 1) * col_orb, :]

        forwards = []
        for k in order:
            block = lax.rem(y + ny - k, ny)
            rows = pl.ds(block * per_block, per_block)
            if k == 0:
                own.wait()
            else:
                send(tensor.at[0], ext.at[core, rows, :, :, middle], a_send.at[k - 1], a_recv.at[k - 1], place()).wait_recv()
            whole = ext.at[core, rows, :, :, middle]
            to_half = block // half
            slot = lax.rem(block, half)
            over = send(whole, whole, c_send.at[k], c_recv.at[block], place(to_core=1 - core))
            left = send(ext.at[core, rows, :, :, pl.ds(rim, rim)], ext.at[core, rows, :, :, pl.ds(rim + length, rim)],
                        hr_send.at[k], hr_recv.at[core, slot], place(to_core=to_half, to_z=z_down))
            right = send(ext.at[core, rows, :, :, pl.ds(length, rim)], ext.at[core, rows, :, :, pl.ds(0, rim)],
                         hl_send.at[k], hl_recv.at[core, slot], place(to_core=to_half, to_z=z_up))
            for copy in (over, left, right):
                copy.start()
                forwards.append(copy)

        d_up.wait()
        d_down.wait()
        for t in range(blocks):
            for e in range(t, t + band):
                rows, cols = part(e, t)
                c = band - 1 - (e - t)
                if e < centre:
                    big[t // 2, rows, cols] = dens_low[c - centre - 1, e * col_orb : (e + 1) * col_orb, :]
                elif e >= centre + blocks:
                    at = e - centre - blocks
                    big[t // 2, rows, cols] = dens_high[c, at * col_orb : (at + 1) * col_orb, :]

        for slot in range(half):
            rows = pl.ds((core * half + slot) * per_block, per_block)
            for source in range(CORES):
                send(ext.at[0, rows, :, :, pl.ds(rim, rim)], ext.at[source, rows, :, :, pl.ds(rim + length, rim)],
                     hr_send.at[0], hr_recv.at[source, slot], place()).wait_recv()
                send(ext.at[0, rows, :, :, pl.ds(rim, rim)], ext.at[source, rows, :, :, pl.ds(0, rim)],
                     hl_send.at[0], hl_recv.at[source, slot], place()).wait_recv()
        for block in range(ny):
            rows = pl.ds(block * per_block, per_block)
            there = ext.at[1 - core, rows, :, :, middle]
            send(there, there, c_send.at[0], c_recv.at[block], place()).wait_recv()

        half_rows = half * per_block
        depth = big.shape[1]
        width = big.shape[2]
        m_rows = mixed.shape[0]
        for source in range(CORES):
            for u in range(big.shape[0]):
                rows = ext[source, pl.ds(core * half_rows, half_rows), :, :, u * width : u * width + depth].reshape(m_rows, depth)
                value = jnp.dot(rows, big[u], preferred_element_type=F32)
                mixed[:, source * length + u * width : source * length + (u + 1) * width] = value.astype(BF16)

        def terms(to):
            total = None
            for source in range(CORES):
                rows = ext[source, :, pl.ds(to, 1), :, rim : rim + length].reshape(-1, length)
                value = lax.dot_general(rows, mixed[:, source * length : (source + 1) * length],
                                        (((1,), (1,)), ((), ())), preferred_element_type=F32)
                total = value if total is None else total + value
            return total

        x_copies = []
        for k in range(1, nx):
            to = lax.rem(x + k, nx)
            x_send[k - 1] = terms(to).astype(BF16).reshape(x_send.shape[1:])
            copy = send(x_send.at[k - 1], x_recv.at[k - 1], xs_sem.at[k - 1], xr_sem.at[k - 1], place(to_x=to))
            copy.start()
            x_copies.append(copy)
        x_own[...] = terms(x).reshape(x_own.shape)
        for k in range(1, nx):
            x_copies[k - 1].wait_recv()
            x_own[...] += x_recv[k - 1].astype(F32)
        z_send[...] = x_own[...].astype(BF16)
        z_copies = []
        for k in range(1, nz):
            to = lax.rem(z + k, nz)
            copy = send(z_send.at[to], z_recv.at[k - 1], zs_sem.at[k - 1], zr_sem.at[k - 1], place(to_z=to))
            copy.start()
            z_copies.append(copy)
        z_sum[...] = x_own[z]
        for k in range(1, nz):
            z_copies[k - 1].wait_recv()
            z_sum[...] += z_recv[k - 1].astype(F32)
        for h in range(half):
            y_send[h] = z_sum[:, h * 128 : (h + 1) * 128]
        for h in range(half):
            to = core * half + h
            offset = lax.rem(to + ny - y, ny)

            @pl.when(to != y)
            def _(h=h, to=to, offset=offset):
                send(y_send.at[h], y_recv.at[offset - 1], ys_sem.at[h], yr_sem.at[offset - 1], place(to_y=to)).start()

        @pl.when(owner == core)
        def _():
            total = y_send[lax.rem(y, half)]
            for k in range(1, ny):
                send(y_send.at[0], y_recv.at[k - 1], ys_sem.at[0], yr_sem.at[k - 1], place()).wait_recv()
            for k in range(1, ny):
                total += y_recv[k - 1]
            gathered[x] = total
            for k in range(1, 2 * nx):
                device = {"ri": lax.rem(ri + k, CORES * nx), "row": y, "col": z}
                send(gathered.at[x], gathered.at[x], bs_sem.at[k - 1], br_sem.at[x], device).start()

        for k in range(nx):
            @pl.when((owner != core) | (k != x))
            def _(k=k):
                send(gathered.at[k], gathered.at[k], bs_sem.at[0], br_sem.at[k], place()).wait_recv()

        out[...] = gathered[...].reshape(out.shape)

        for copy in started:
            copy.wait_send()
        for copy in forwards:
            copy.wait_send()
        for copy in x_copies:
            copy.wait_send()
        for copy in z_copies:
            copy.wait_send()
        for h in range(half):
            @pl.when(core * half + h != y)
            def _(h=h):
                send(y_send.at[h], y_recv.at[0], ys_sem.at[h], yr_sem.at[0], place()).wait_send()

        @pl.when(owner == core)
        def _():
            for k in range(1, 2 * nx):
                send(gathered.at[x], gathered.at[x], bs_sem.at[k - 1], br_sem.at[x], place()).wait_send()

    return kernel


def solution(mesh):
    nx = mesh.shape["ri"] // CORES
    ny = mesh.shape["row"]
    nz = mesh.shape["col"]

    def per_device(three_centre, density_band, band_mask):
        funcs, block_rows, length = three_centre.shape
        blocks, band = band_mask.shape
        col_orb = density_band.shape[2]
        rows = block_rows * ny
        run = rows // (nz * nx)
        per_block = nz // ny
        centre = band // 2
        rim = centre * col_orb
        m_rows = rows // CORES
        half = ny // CORES
        tensor = three_centre.reshape(funcs, per_block, nx, run, length)
        density = jnp.transpose(density_band, (1, 0, 2))
        dma = pltpu.SemaphoreType.DMA
        return pl.pallas_call(
            make_kernel(nx, ny, nz, col_orb, blocks, band),
            out_shape=jax.ShapeDtypeStruct((rows // nz, block_rows), F32),
            in_specs=[
                pl.BlockSpec(memory_space=pl.ANY),
                pl.BlockSpec(memory_space=pl.ANY),
                pl.BlockSpec(memory_space=pltpu.SMEM),
            ],
            out_specs=pl.BlockSpec(memory_space=pltpu.VMEM),
            scratch_shapes=[
                pltpu.VMEM((CORES, nz, nx, run, length + 2 * rim), BF16),
                pltpu.VMEM(density.shape, BF16),
                pltpu.VMEM((centre, rim, col_orb), BF16),
                pltpu.VMEM((centre, rim, col_orb), BF16),
                pltpu.VMEM((blocks // 2, (band + 1) * col_orb, 2 * col_orb), BF16),
                pltpu.VMEM((m_rows, CORES * length), BF16),
                pltpu.VMEM((nz, run, m_rows), F32),
                pltpu.VMEM((nx - 1, nz, run, m_rows), BF16),
                pltpu.VMEM((nx - 1, nz, run, m_rows), BF16),
                pltpu.VMEM((nz, run, m_rows), BF16),
                pltpu.VMEM((nz - 1, run, m_rows), BF16),
                pltpu.VMEM((run, m_rows), F32),
                pltpu.VMEM((half, run, block_rows), F32),
                pltpu.VMEM((ny - 1, run, block_rows), F32),
                pltpu.VMEM((nx, run, block_rows), F32),
                dma, dma((ny - 1,)), dma((ny - 1,)), dma((ny,)), dma((ny,)),
                dma((ny,)), dma((CORES, half)), dma((ny,)), dma((CORES, half)),
                dma, dma, dma, dma, dma,
                dma((nx - 1,)), dma((nx - 1,)), dma((nz - 1,)), dma((nz - 1,)),
                dma((half,)), dma((ny - 1,)), dma((2 * nx - 1,)), dma((nx,)),
            ],
            compiler_params=pltpu.CompilerParams(
                collective_id=0, has_side_effects=True, vmem_limit_bytes=48 * 1024 * 1024
            ),
        )(tensor, density, band_mask)

    placed = (P("ri", "row", "col"), P("col", None, None), P("col", None))
    return jax.shard_map(
        per_device, mesh=mesh, in_specs=placed, out_specs=P("col", "row"), check_vma=False
    )
```

time: 233 us -> 94.6 us (0.41)
  waiting for transfers between devices: 160 us -> 0 us
  Pallas kernels: 0 us -> 90.7 us
  blocking collectives: 32.9 us -> 0 us
  between operations: 13.5 us -> 0.01 us
  matrix products: 10.2 us -> 0 us
  starting transfers between devices: 7.94 us -> 0 us
  other arithmetic: 2.81 us -> 0 us
    pallas_call x0 -> x1, Pallas kernels: none -> 90.7 us  [per_device(): pl.pallas_call(make_kernel(nx, ny, nz, col_orb, blocks, band), out_shape=...]
    unnamed x3 -> x0, waiting for transfers between devices: 63.1 us -> none
    ppermute x2 -> x0, waiting for transfers between devices: 59.2 us -> none  [from_behind(): lax.ppermute(shard, axis, [(i, (i + by) % length) for i in range(length)])]
    all_gather x1 -> x0, waiting for transfers between devices: 37.9 us -> none  [per_device(): lax.all_gather(three_centre, 'row', axis=1, tiled=True)]
    psum x1 -> x0, blocking collectives: 32.9 us -> none  [per_device(): return lax.psum(summed, 'ri')]
    dot_general x6 -> x0, matrix products: 10.2 us -> none  [the longest x1 6.25 us: per_device(): jnp.einsum('pns,pms->nm', lax.all_gather(three_centre, 'row', axis=1, til...]
    ppermute x2 -> x0, starting transfers between devices: 7.9 us -> none  [from_behind(): lax.ppermute(shard, axis, [(i, (i + by) % length) for i in range(length)])]
    convert_element_type x3 -> x0, other arithmetic: 2.33 us -> none  [the longest x1 1.49 us: per_device(): (density_band.astype(jnp.float32) * weights[:, :, None]).astype(jnp.bfloa...]
  transfers between devices with their start and end apart: 4 -> 0, of which waited for: 4 -> 0; matrix products, arithmetic and copies ran while one was open for 3% -> 0% of each run, Pallas kernels for 0% -> 0%
where the time goes in v1:
time: 94.6 us; the launch traced here: 94.4 us
  Pallas kernels  90.7 us (96%)
  local copies, waits for them, and re-layouts  3.61 us (4%)
    pallas_call x1, Pallas kernels, per_device(): pl.pallas_call(make_kernel(nx, ny, nz, col_orb, blocks, band), out_shape=...  90.7 us
    unnamed x7, local copies, waits for them, and re-layouts  3.61 us

profile of v1, /device:TPU:1, one launch (start us, length us, event | category | flops | bytes accessed | tf_op | source)
XLA Modules:
  0.0 94.4 jit_solution(9945830345350211459)
XLA Ops:
  0.0 0.0 copy-start.2
  0.0 0.7 copy-done.2
  0.7 0.0 copy-start
  0.7 1.2 %copy-done = bf16[8,128,512]{2,1,0:T(8,128)(2,1)S(1)} copy-done((bf16[8,128,512]{2,1,0:T(8,128)(2,1)S(1)}, bf16[8,128,512]{2,1,0:T(8,128)(2,1)}, u32[]{:S(2)}) %copy-start) | copy-done | bytes 1048600
  1.9 0.0 copy-start.1
  1.9 1.1 %copy-done.1 = bf16[512,5,128]{2,0,1:T(8,128)(2,1)S(1)} copy-done((bf16[512,5,128]{2,0,1:T(8,128)(2,1)S(1)}, bf16[512,5,128]{2,0,1:T(8,128)(2,1)}, u32[]{:S(2)}) %copy-start.1) | copy-done | bytes 655384
  3.0 90.7 %shard_map.37 = f32[64,128]{1,0:T(8,128)S(1)} custom-call(bf16[8,2,4,16,512]{4,3,2,1,0:T(8,128)(2,1)S(1)} %bitcast.2, bf16[5,512,128]{2,1,0:T(8,128)(2,1)S(1)} %bitcast.3, s32[4,5]{1,0:T(4,128)S(1)} %copy-done.2), custom_call_target="tpu_custom_call" | custom-call | tf_op jit(solution)/shard_map/pallas_call | solution.py:257
  93.7 0.6 copy.5
Async XLA Ops:
  0.0 0.7 copy-start.2
  0.7 1.2 %copy-start = (bf16[8,128,512]{2,1,0:T(8,128)(2,1)S(1)}, bf16[8,128,512]{2,1,0:T(8,128)(2,1)}, u32[]{:S(2)}) copy-start(bf16[8,128,512]{2,1,0:T(8,128)(2,1)} %param.3) | copy-start | bytes 3145732
  1.9 1.1 %copy-start.1 = (bf16[512,5,128]{2,0,1:T(8,128)(2,1)S(1)}, bf16[512,5,128]{2,0,1:T(8,128)(2,1)}, u32[]{:S(2)}) copy-start(bf16[512,5,128]{2,0,1:T(8,128)(2,1)} %param.4) | copy-start | bytes 1966084

commit v2 on v0

v2 whole, which is shorter than its diff:
```python
import jax
import jax.numpy as jnp
from jax import lax
from jax.experimental import pallas as pl
from jax.experimental.pallas import tpu as pltpu
from jax.sharding import PartitionSpec as P

CORES = 2
BF16 = jnp.bfloat16
F32 = jnp.float32
MESH = pl.DeviceIdType.MESH


def remote(source, target, send_sem, recv_sem, device):
    return pltpu.make_async_remote_copy(
        src_ref=source, dst_ref=target, send_sem=send_sem, recv_sem=recv_sem,
        device_id=device, device_id_type=MESH,
    )


def make_kernel(nx, ny, nz, col_orb, blocks, band):
    centre = band // 2
    rim = centre * col_orb
    length = blocks * col_orb
    half = ny // CORES
    order = [0]
    for step in range(1, half):
        order += [step, ny - step]
    order.append(half)
    phases = [[0]] + [[2 * p - 1, 2 * p] for p in range(1, half)] + [[ny - 1]]

    def column_slot(offset):
        return (0, offset) if offset < half else (1, ny - 1 - offset)

    slot_at = {column_slot(offset): at for at, offset in enumerate(order)}

    def reach(p):
        rows = ny if p >= half else max(1 + 2 * p, 0)
        return rows, (min(max(p + 1, 0), half), max(p, 0))

    early = reach(half - 2)[0]

    def parts(side):
        found = []
        rows, slots = 0, 0
        for p in (half - 2, half - 1, half):
            now, upto = reach(p)
            upto = upto[side]
            found.append(((max(rows, early), now), (0, 0), (rows, now, 0, slots)))
            found.append(((0, 0), (slots, upto), (0, now, slots, upto)))
            rows, slots = now, upto
        return found

    def used(region):
        return region[1] > region[0] and region[3] > region[2]

    rounds = []
    while 2 ** len(rounds) < nz // 2:
        rounds.append(2 ** len(rounds))

    def kernel(
        tensor, density, band_mask, out,
        mask, ext, dens, dens_low, dens_high, big, mixed,
        x_own, x_send, x_recv, z_send, z_recv, y_send, y_recv, gathered,
        mask_sem, own_sem, a_send, a_recv, c_send, c_recv, h_send, h_recv, d_sem, d_send, d_recv,
        xs_sem, xr_sem, zs_sem, zr_sem, ys_sem, yr_sem, bs_sem, br_sem, far,
    ):
        state = []

        def phase(name):
            pass

        ri = lax.axis_index("ri")
        y = lax.axis_index("row")
        z = lax.axis_index("col")
        x = ri // CORES
        core = lax.rem(ri, CORES)
        per_block = tensor.shape[1]

        def place(to_x=x, to_core=core, to_y=y, to_z=z):
            return {"ri": to_x * CORES + to_core, "row": to_y, "col": to_z}

        z_up = lax.rem(z + 1, nz)
        z_down = lax.rem(z + nz - 1, nz)

        phase("p0_prep")
        barrier = pltpu.get_barrier_semaphore()
        partners = [place(to_y=lax.rem(y + k, ny)) for k in range(1, ny)]
        partners += [place(to_core=1 - core)]
        for k in range(1, nx):
            partners += [place(lax.rem(x + k, nx), flip) for flip in (core, 1 - core)]
        partners += [place(to_core=flip, to_z=to) for flip in (core, 1 - core) for to in (z_up, z_down)]
        for partner in partners:
            pl.semaphore_signal(barrier, inc=1, device_id=partner, device_id_type=MESH)

        load = pltpu.make_async_copy(density, dens, d_sem)
        load.start()
        masks = pltpu.make_async_copy(band_mask, mask, mask_sem)
        masks.start()
        middle = pl.ds(rim, length)
        own = pltpu.make_async_copy(tensor.at[y], ext.at[core, 0, :, :, :, middle], own_sem)
        own.start()
        big[...] = jnp.zeros_like(big)
        load.wait()
        masks.wait()
        for b in range(blocks):
            for c in range(band):
                weight = mask[b, c].astype(F32)
                rows = slice(b * col_orb, (b + 1) * col_orb)
                dens[c, rows, :] = (dens[c, rows, :].astype(F32) * weight).astype(BF16)
        phase("p1_barrier")
        pl.semaphore_wait(barrier, len(partners))
        phase("p2_start")

        def far_signal(r):
            for side, to in ((0, lax.rem(z + nz - rounds[r], nz)), (1, lax.rem(z + rounds[r], nz))):
                pl.semaphore_signal(far.at[r, side], inc=1, device_id=place(to_z=to), device_id_type=MESH)

        def far_wait(r):
            for side in range(2):
                pl.semaphore_wait(far.at[r, side], 1)

        started = [None]
        for at in range(1, ny):
            to = lax.rem(y + ny - order[at], ny)
            started.append(remote(tensor.at[to], ext.at[core, at, :, :, :, middle], a_send, a_recv.at[at - 1], place(to_y=to)))

        def begin(p):
            if 0 < p <= half:
                for at in phases[p]:
                    started[at].start()

        begin(1)
        begin(2)
        d_up = remote(dens.at[pl.ds(centre + 1, centre), pl.ds(length - rim, rim)], dens_low, d_send, d_recv, place(to_z=z_up))
        d_down = remote(dens.at[pl.ds(0, centre), pl.ds(0, rim)], dens_high, d_send, d_recv, place(to_z=z_down))
        d_up.start()
        d_down.start()
        if rounds:
            far_signal(0)

        def tile(e, t):
            row, col = e - 2 * (t // 2), t % 2
            return slice(row * col_orb, (row + 1) * col_orb), slice(col * col_orb, (col + 1) * col_orb)

        for t in range(blocks):
            for e in range(max(t, centre), min(t + band, centre + blocks)):
                rows, cols = tile(e, t)
                local = e - centre
                big[t // 2, rows, cols] = dens[band - 1 - (e - t), local * col_orb : (local + 1) * col_orb, :]

        def halo_copies(at, source):
            side, slot = column_slot(order[at])
            left = remote(ext.at[source, at, :, :, :, pl.ds(rim, rim)], ext.at[source, at, :, :, :, pl.ds(rim + length, rim)],
                          h_send, h_recv.at[slot], place(to_core=side, to_z=z_down))
            right = remote(ext.at[source, at, :, :, :, pl.ds(length, rim)], ext.at[source, at, :, :, :, pl.ds(0, rim)],
                           h_send, h_recv.at[slot], place(to_core=side, to_z=z_up))
            return left, right

        def over_copy(at, source):
            whole = ext.at[source, at, :, :, :, middle]
            return remote(whole, whole, c_send, c_recv.at[at], place(to_core=1 - core))

        def forward(p):
            for at in phases[p]:
                phase(f"p3_arrive{at}")
                if at == 0:
                    own.wait()
                else:
                    started[at].wait_recv()
                for copy in (*halo_copies(at, core), over_copy(at, core)):
                    copy.start()

        def density_rims():
            both = dens.at[pl.ds(0, centre), pl.ds(0, 2 * rim)]
            remote(both, both, d_send, d_recv, place()).wait()
            for t in range(blocks):
                for e in range(t, t + band):
                    rows, cols = tile(e, t)
                    c = band - 1 - (e - t)
                    if e < centre:
                        big[t // 2, rows, cols] = dens_low[c - centre - 1, e * col_orb : (e + 1) * col_orb, :]
                    elif e >= centre + blocks:
                        to = e - centre - blocks
                        big[t // 2, rows, cols] = dens_high[c, to * col_orb : (to + 1) * col_orb, :]

        depth = big.shape[1]
        width = big.shape[2]

        def mix(side, slot):
            at = slot_at[side, slot]
            for source in range(CORES):
                for u in range(big.shape[0]):
                    rows = ext[source, at, :, :, :, u * width : u * width + depth].reshape(-1, depth)
                    value = jnp.dot(rows, big[u], preferred_element_type=F32)
                    at_row = source * length + u * width
                    mixed[at_row : at_row + width, slot * 128 : (slot + 1) * 128] = value.T.astype(BF16)

        def terms(region):
            n0, n1, m0, m1 = region
            total = None
            for source in range(CORES):
                rows = ext[source, n0:n1, :, :, :, rim : rim + length].reshape(-1, length)
                value = jnp.dot(rows, mixed[source * length : (source + 1) * length, m0 * 128 : m1 * 128], preferred_element_type=F32)
                total = value if total is None else total + value
            total = total.reshape(n1 - n0, per_block, nx, -1, (m1 - m0) * 128)
            kept = None
            for to in range(nx):
                value = total[:, :, to]
                x_send[to, n0:n1, :, :, m0 * 128 : m1 * 128] = value.astype(BF16)
                kept = value if kept is None else jnp.where(x == to, value, kept)
            x_own[n0:n1, :, :, m0 * 128 : m1 * 128] = kept

        def x_copy(k, part, region):
            n0, n1, m0, m1 = region
            at = (pl.ds(n0, n1 - n0), slice(None), slice(None), pl.ds(m0 * 128, (m1 - m0) * 128))
            to = lax.rem(x + k, nx)
            return remote(x_send.at[(to, *at)], x_recv.at[(k - 1, *at)], xs_sem, xr_sem.at[part],
                          place(to_x=to))

        def advance(*chosen):
            for side in range(CORES):
                @pl.when(core == side)
                def _(side=side):
                    for part in chosen:
                        arrived, mixing, region = parts(side)[part]
                        for slot in range(*mixing):
                            rims = ext.at[:, slot_at[side, slot], :, :, :, pl.ds(0, 2 * rim)]
                            remote(rims, rims, h_send, h_recv.at[slot], place()).wait_recv()
                        for at in range(*arrived):
                            over_copy(at, 1 - side).wait_recv()
                        for slot in range(*mixing):
                            mix(side, slot)
                        if not used(region):
                            continue
                        terms(region)
                        for k in range(1, nx):
                            x_copy(k, part, region).start()

        sent, waited = 1, 0
        for p in range(max(half - 1, 0)):
            forward(p)
            for at in phases[p]:
                over_copy(at, 1 - core).wait_recv()
            if p > 0:
                begin(p + 2)
            if 1 <= p < len(rounds):
                far_wait(p - 1)
                far_signal(p)
                sent, waited = p + 1, p
        density_rims()
        def z_copy(part, region, at, b):
            lanes = pl.ds(region[2] * 128, (region[3] - region[2]) * 128)
            to = lax.rem(y + order[at], ny) * per_block + b
            k = lax.rem(to + nz - z, nz)
            slot = lax.rem(k + nz - 1, nz)
            return k, remote(z_send.at[to, :, lanes], z_recv.at[slot, :, lanes], zs_sem, zr_sem,
                             place(to_z=to))

        def settle(*chosen):
            for side in range(CORES):
                @pl.when(core == side)
                def _(side=side):
                    for part in chosen:
                        region = parts(side)[part][2]
                        if not used(region):
                            continue
                        n0, n1, m0, m1 = region
                        lanes = pl.ds(m0 * 128, (m1 - m0) * 128)
                        landed = x_recv.at[:, pl.ds(n0, n1 - n0), :, :, lanes]
                        remote(landed, landed, xs_sem, xr_sem.at[part], place()).wait_recv()
                        for at in range(n0, n1):
                            total = x_own[at, :, :, lanes]
                            for k in range(1, nx):
                                total += x_recv[k - 1, at, :, :, lanes].astype(F32)
                            block = lax.rem(y + order[at], ny)
                            x_own[at, :, :, lanes] = total
                            z_send[pl.ds(block * per_block, per_block), :, lanes] = total.astype(BF16)

                            @pl.when(block == z // per_block)
                            def _(at=at, lanes=lanes):
                                y_send[:, lanes] = x_own[at, lax.rem(z, per_block), :, lanes]
                        for at in range(n0, n1):
                            for b in range(per_block):
                                k, copy = z_copy(part, region, at, b)

                                @pl.when(k != 0)
                                def _(copy=copy):
                                    copy.start()

        phase("p4_a")
        advance(0, 1)
        forward(half - 1)
        phase("p4_b1")
        advance(2)
        for r in range(waited, len(rounds)):
            if r >= sent:
                far_signal(r)
            far_wait(r)
        phase("p5_za")
        settle(0, 1)
        phase("p4_b2")
        advance(3)
        forward(half)
        phase("p4_c1")
        advance(4)
        phase("p4_c2")
        advance(5)
        phase("p5_zb")
        settle(2, 3)
        phase("p5_zc")
        settle(4, 5)
        phase("p7_zwait")
        landed = z_recv.at[pl.ds(0, nz - 1)]
        remote(landed, landed, zs_sem, zr_sem, place()).wait_recv()
        total = y_send[...]
        for slot in range(nz - 1):
            total += z_recv[slot].astype(F32)
        for slot in range(half):
            y_recv[half + slot] = total[:, slot * 128 : (slot + 1) * 128]
        phase("p8_ywait")

        def y_copy(slot):
            to = lax.rem(y + core * (ny - 1) + slot * (1 - 2 * core), ny)
            return remote(y_recv.at[half + slot], y_recv.at[slot], ys_sem, yr_sem, place(to_y=to))

        def y_all(side):
            whole = y_recv.at[pl.ds(0, half - 1 + side)]
            return remote(whole, whole, ys_sem, yr_sem, place())

        for slot in range(1, half):
            y_copy(slot).start()
        for side in range(CORES):
            @pl.when(core == side)
            def _(side=side):
                if side == 1:
                    y_copy(0).start()
                if half - 1 + side > 0:
                    y_all(side).wait_recv()
                if side == 0:
                    y_recv[0] = y_recv[half]

        total = y_recv[0]
        for slot in range(1, half):
            total += y_recv[slot]
        gathered[ri] = total
        phase("p9_bwait")

        def b_copy(k, source):
            device = {"ri": lax.rem(ri + k, CORES * nx), "row": y, "col": z}
            return remote(gathered.at[source], gathered.at[source], bs_sem, br_sem, device)

        for k in range(1, CORES * nx):
            b_copy(k, ri).start()
        spread = gathered.at[pl.ds(0, CORES * nx - 1)]
        remote(spread, spread, bs_sem, br_sem, place()).wait_recv()
        run = gathered.shape[1]
        for k in range(nx):
            out[k * run : (k + 1) * run, :] = gathered[CORES * k] + gathered[CORES * k + 1]
        phase("pa_end")

        for view, sem in (
            (ext.at[core, pl.ds(1, ny - 1), :, :, :, middle], a_send),
            (ext.at[core, :, :, :, :, middle], c_send),
            (ext.at[core, :, :, :, :, pl.ds(0, 2 * rim)], h_send),
            (x_send.at[pl.ds(0, nx - 1)], xs_sem),
            (z_send.at[pl.ds(0, nz - 1)], zs_sem),
            (spread, bs_sem),
        ):
            remote(view, view, sem, sem, place()).wait_send()
        for side in range(CORES):
            @pl.when(core == side)
            def _(side=side):
                if half - 1 + side > 0:
                    y_all(side).wait_send()
        phase(None)

    return kernel, max(len(rounds), 1)


def solution(mesh):
    nx = mesh.shape["ri"] // CORES
    ny = mesh.shape["row"]
    nz = mesh.shape["col"]

    def per_device(three_centre, density_band, band_mask):
        funcs, block_rows, length = three_centre.shape
        blocks, band = band_mask.shape
        col_orb = density_band.shape[2]
        rows = block_rows * ny
        run = rows // (nz * nx)
        per_block = nz // ny
        centre = band // 2
        rim = centre * col_orb
        half = ny // CORES
        m_rows = half * block_rows
        tensor = three_centre.reshape(funcs, per_block, nx, run, length)
        density = jnp.transpose(density_band, (1, 0, 2))
        dma = pltpu.SemaphoreType.DMA
        kernel, rounds = make_kernel(nx, ny, nz, col_orb, blocks, band)
        return pl.pallas_call(
            kernel,
            out_shape=jax.ShapeDtypeStruct((rows // nz, block_rows), F32),
            in_specs=[
                pl.BlockSpec(memory_space=pltpu.HBM),
                pl.BlockSpec(memory_space=pltpu.HBM),
                pl.BlockSpec(memory_space=pltpu.HBM),
            ],
            out_specs=pl.BlockSpec(memory_space=pltpu.VMEM),
            scratch_shapes=[
                pltpu.SMEM((blocks, band), jnp.int32),
                pltpu.VMEM((CORES, ny, per_block, nx, run, length + 2 * rim), BF16),
                pltpu.VMEM(density.shape, BF16),
                pltpu.VMEM((centre, rim, col_orb), BF16),
                pltpu.VMEM((centre, rim, col_orb), BF16),
                pltpu.VMEM((blocks // 2, (band + 1) * col_orb, 2 * col_orb), BF16),
                pltpu.VMEM((CORES * length, m_rows), BF16),
                pltpu.VMEM((ny, per_block, run, m_rows), F32),
                pltpu.VMEM((nx, ny, per_block, run, m_rows), BF16),
                pltpu.VMEM((nx - 1, ny, per_block, run, m_rows), BF16),
                pltpu.VMEM((nz, run, m_rows), BF16),
                pltpu.VMEM((nz, run, m_rows), BF16),
                pltpu.VMEM((run, m_rows), F32),
                pltpu.VMEM((2 * half, run, block_rows), F32),
                pltpu.VMEM((CORES * nx, run, block_rows), F32),
                dma, dma, dma, dma((ny - 1,)), dma, dma((ny,)), dma, dma((half,)), dma, dma, dma,
                dma, dma((6,)), dma, dma, dma, dma, dma, dma,
                pltpu.SemaphoreType.REGULAR((rounds, 2)),
            ],
            compiler_params=pltpu.CompilerParams(
                collective_id=0, has_side_effects=True, vmem_limit_bytes=67043328
            ),
        )(tensor, density, band_mask)

    placed = (P("ri", "row", "col"), P("col", None, None), P("col", None))
    return jax.shard_map(
        per_device, mesh=mesh, in_specs=placed, out_specs=P("col", "row"), check_vma=False
    )
```

time: 233 us -> 79.2 us (0.34)
  waiting for transfers between devices: 160 us -> 0 us
  Pallas kernels: 0 us -> 77.6 us
  blocking collectives: 32.9 us -> 0 us
  between operations: 13.5 us -> 0.01 us
  matrix products: 10.2 us -> 0 us
  starting transfers between devices: 7.94 us -> 0 us
  other arithmetic: 2.81 us -> 0 us
    pallas_call x0 -> x1, Pallas kernels: none -> 77.6 us  [per_device(): pl.pallas_call(kernel, out_shape=jax.ShapeDtypeStruct((rows // nz, block_...]
    unnamed x3 -> x0, waiting for transfers between devices: 63.1 us -> none
    ppermute x2 -> x0, waiting for transfers between devices: 59.2 us -> none  [from_behind(): lax.ppermute(shard, axis, [(i, (i + by) % length) for i in range(length)])]
    all_gather x1 -> x0, waiting for transfers between devices: 37.9 us -> none  [per_device(): lax.all_gather(three_centre, 'row', axis=1, tiled=True)]
    psum x1 -> x0, blocking collectives: 32.9 us -> none  [per_device(): return lax.psum(summed, 'ri')]
    dot_general x6 -> x0, matrix products: 10.2 us -> none  [the longest x1 6.25 us: per_device(): jnp.einsum('pns,pms->nm', lax.all_gather(three_centre, 'row', axis=1, til...]
    ppermute x2 -> x0, starting transfers between devices: 7.9 us -> none  [from_behind(): lax.ppermute(shard, axis, [(i, (i + by) % length) for i in range(length)])]
    convert_element_type x3 -> x0, other arithmetic: 2.33 us -> none  [the longest x1 1.49 us: per_device(): (density_band.astype(jnp.float32) * weights[:, :, None]).astype(jnp.bfloa...]
  transfers between devices with their start and end apart: 4 -> 0, of which waited for: 4 -> 0; matrix products, arithmetic and copies ran while one was open for 3% -> 0% of each run, Pallas kernels for 0% -> 0%
where the time goes in v2:
time: 79.2 us; the launch traced here: 79 us
  Pallas kernels  77.6 us (98%)
  local copies, waits for them, and re-layouts  1.38 us (2%)
    pallas_call x1, Pallas kernels, per_device(): pl.pallas_call(kernel, out_shape=jax.ShapeDtypeStruct((rows // nz, block_...  77.6 us

profile of v2, /device:TPU:1, one launch (start us, length us, event | category | flops | bytes accessed | tf_op | source)
XLA Modules:
  0.0 79.0 jit_solution(13685727866361358664)
XLA Ops:
  0.0 77.6 %shard_map.37 = f32[64,128]{1,0:T(8,128)} custom-call(bf16[8,2,4,16,512]{4,3,2,1,0:T(8,128)(2,1)} %bitcast.2, bf16[5,512,128]{2,1,0:T(8,128)(2,1)} %bitcast.3, s32[4,5]{1,0:T(4,128)} %band_mask.1), custom_call_target="tpu_custom_call" | custom-call | tf_op jit(solution)/shard_map/pallas_call | solution.py:401
  77.6 1.4 %copy.5 = f32[64,128]{1,0:T(8,128)} copy(f32[64,128]{1,0:T(8,128)} %shard_map.37) | data formatting | bytes 65536

commit v3 on v2

--- a/solution.py
+++ b/solution.py
@@ -43,10 +43,10 @@
     def parts(side):
         found = []
         rows, slots = 0, 0
-        for p in (half - 2, half - 1, half):
+        for p in (half - 3, half - 2, half - 1, half):
             now, upto = reach(p)
             upto = upto[side]
-            found.append(((max(rows, early), now), (0, 0), (rows, now, 0, slots)))
+            found.append(((max(rows, early), max(now, early)), (0, 0), (rows, now, 0, slots)))
             found.append(((0, 0), (slots, upto), (0, now, slots, upto)))
             rows, slots = now, upto
         return found
@@ -101,6 +101,30 @@
         own = pltpu.make_async_copy(tensor.at[y], ext.at[core, 0, :, :, :, middle], own_sem)
         own.start()
         big[...] = jnp.zeros_like(big)
+        phase("p1_barrier")
+        pl.semaphore_wait(barrier, len(partners))
+        phase("p2_start")
+
+        def far_signal(r):
+            for side, to in ((0, lax.rem(z + nz - rounds[r], nz)), (1, lax.rem(z + rounds[r], nz))):
+                pl.semaphore_signal(far.at[r, side], inc=1, device_id=place(to_z=to), device_id_type=MESH)
+
+        def far_wait(r):
+            for side in range(2):
+                pl.semaphore_wait(far.at[r, side], 1)
+
+        started = [None]
+        for at in range(1, ny):
+            to = lax.rem(y + ny - order[at], ny)
+            started.append(remote(tensor.at[to], ext.at[core, at, :, :, :, middle], a_send, a_recv.at[at - 1], place(to_y=to)))
+
+        def begin(p):
+            if 0 < p <= half:
+                for at in phases[p]:
+                    started[at].start()
+
+        begin(1)
+        begin(2)
         load.wait()
         masks.wait()
         for b in range(blocks):
@@ -108,30 +132,6 @@
                 weight = mask[b, c].astype(F32)
                 rows = slice(b * col_orb, (b + 1) * col_orb)
                 dens[c, rows, :] = (dens[c, rows, :].astype(F32) * weight).astype(BF16)
-        phase("p1_barrier")
-        pl.semaphore_wait(barrier, len(partners))
-        phase("p2_start")
-
-        def far_signal(r):
-            for side, to in ((0, lax.rem(z + nz - rounds[r], nz)), (1, lax.rem(z + rounds[r], nz))):
-                pl.semaphore_signal(far.at[r, side], inc=1, device_id=place(to_z=to), device_id_type=MESH)
-
-        def far_wait(r):
-            for side in range(2):
-                pl.semaphore_wait(far.at[r, side], 1)
-
-        started = [None]
-        for at in range(1, ny):
-            to = lax.rem(y + ny - order[at], ny)
-            started.append(remote(tensor.at[to], ext.at[core, at, :, :, :, middle], a_send, a_recv.at[at - 1], place(to_y=to)))
-
-        def begin(p):
-            if 0 < p <= half:
-                for at in phases[p]:
-                    started[at].start()
-
-        begin(1)
-        begin(2)
         d_up = remote(dens.at[pl.ds(centre + 1, centre), pl.ds(length - rim, rim)], dens_low, d_send, d_recv, place(to_z=z_up))
         d_down = remote(dens.at[pl.ds(0, centre), pl.ds(0, rim)], dens_high, d_send, d_recv, place(to_z=z_down))
         d_up.start()
@@ -237,18 +237,6 @@
                         for k in range(1, nx):
                             x_copy(k, part, region).start()
 
-        sent, waited = 1, 0
-        for p in range(max(half - 1, 0)):
-            forward(p)
-            for at in phases[p]:
-                over_copy(at, 1 - core).wait_recv()
-            if p > 0:
-                begin(p + 2)
-            if 1 <= p < len(rounds):
-                far_wait(p - 1)
-                far_signal(p)
-                sent, waited = p + 1, p
-        density_rims()
         def z_copy(part, region, at, b):
             lanes = pl.ds(region[2] * 128, (region[3] - region[2]) * 128)
             to = lax.rem(y + order[at], ny) * per_block + b
@@ -288,28 +276,48 @@
                                 def _(copy=copy):
                                     copy.start()
 
-        phase("p4_a")
-        advance(0, 1)
+        sent, waited = 1, 0
+        for p in range(max(half - 1, 0)):
+            forward(p)
+            if p == half - 2:
+                density_rims()
+                phase("p4_a0")
+                advance(0, 1)
+                phase("p4_over")
+            for at in phases[p]:
+                over_copy(at, 1 - core).wait_recv()
+            if 0 < p < half - 2:
+                begin(p + 2)
+            if 1 <= p < len(rounds):
+                far_wait(p - 1)
+                far_signal(p)
+                sent, waited = p + 1, p
+        if half == 1:
+            density_rims()
+        phase("p4_a1")
+        advance(2, 3)
         forward(half - 1)
+        if half > 2:
+            begin(half)
         phase("p4_b1")
-        advance(2)
+        advance(4)
         for r in range(waited, len(rounds)):
             if r >= sent:
                 far_signal(r)
             far_wait(r)
         phase("p5_za")
-        settle(0, 1)
+        settle(0, 1, 2, 3)
         phase("p4_b2")
-        advance(3)
+        advance(5)
         forward(half)
         phase("p4_c1")
-        advance(4)
+        advance(6)
         phase("p4_c2")
-        advance(5)
+        advance(7)
         phase("p5_zb")
-        settle(2, 3)
+        settle(4, 5)
         phase("p5_zc")
-        settle(4, 5)
+        settle(6, 7)
         phase("p7_zwait")
         landed = z_recv.at[pl.ds(0, nz - 1)]
         remote(landed, landed, zs_sem, zr_sem, place()).wait_recv()
@@ -424,13 +432,13 @@
                 pltpu.VMEM((2 * half, run, block_rows), F32),
                 pltpu.VMEM((CORES * nx, run, block_rows), F32),
                 dma, dma, dma, dma((ny - 1,)), dma, dma((ny,)), dma, dma((half,)), dma, dma, dma,
-                dma, dma((6,)), dma, dma, dma, dma, dma, dma,
+                dma, dma((8,)), dma, dma, dma, dma, dma, dma,
                 pltpu.SemaphoreType.REGULAR((rounds, 2)),
             ],
             compiler_params=pltpu.CompilerParams(
-                collective_id=0, has_side_effects=True, vmem_limit_bytes=67043328
+                collective_id=0, has_side_effects=True, vmem_limit_bytes=48 * 1024 * 1024
             ),
-        )(tensor, density, band_mask)
+        )(*(pltpu.with_memory_space_constraint(operand, pltpu.HBM) for operand in (tensor, density, band_mask)))
 
     placed = (P("ri", "row", "col"), P("col", None, None), P("col", None))
     return jax.shard_map(

time: 79.2 us -> 75 us (0.947)
  Pallas kernels: 77.6 us -> 74.3 us
    pallas_call x1, Pallas kernels: 77.6 us -> 74.3 us  [per_device(): pl.pallas_call(kernel, out_shape=jax.ShapeDtypeStruct((rows // nz, block_...]
where the time goes in v3:
time: 75 us; the launch traced here: 74.9 us
  Pallas kernels  74.3 us (99%)
    pallas_call x1, Pallas kernels, per_device(): pl.pallas_call(kernel, out_shape=jax.ShapeDtypeStruct((rows // nz, block_...  74.3 us

profile of v3, /device:TPU:1, one launch (start us, length us, event | category | flops | bytes accessed | tf_op | source)
XLA Modules:
  0.0 74.9 jit_solution(92152640000944879)
XLA Ops:
  0.0 74.3 %shard_map.37 = f32[64,128]{1,0:T(8,128)S(1)} custom-call(bf16[8,2,4,16,512]{4,3,2,1,0:T(8,128)(2,1)} %bitcast.2, bf16[5,512,128]{2,1,0:T(8,128)(2,1)} %bitcast.3, s32[4,5]{1,0:T(4,128)} %band_mask.1), custom_call_target="tpu_custom_call" | custom-call | tf_op jit(solution)/shard_map/pallas_call | solution.py:409
  74.3 0.6 copy.5

commit v4 on v3

--- a/solution.py
+++ b/solution.py
@@ -268,13 +268,16 @@
                             @pl.when(block == z // per_block)
                             def _(at=at, lanes=lanes):
                                 y_send[:, lanes] = x_own[at, lax.rem(z, per_block), :, lanes]
-                        for at in range(n0, n1):
-                            for b in range(per_block):
-                                k, copy = z_copy(part, region, at, b)
-
-                                @pl.when(k != 0)
-                                def _(copy=copy):
-                                    copy.start()
+                        for near in (False, True):
+                            for at in range(n0, n1):
+                                for b in range(per_block):
+                                    k, copy = z_copy(part, region, at, b)
+                                    close = (k <= nz // 4) | (k >= nz - nz // 4)
+                                    wanted = (k != 0) & close if near else jnp.logical_not(close)
+
+                                    @pl.when(wanted)
+                                    def _(copy=copy):
+                                        copy.start()
 
         sent, waited = 1, 0
         for p in range(max(half - 1, 0)):

time: 75 us -> 74.4 us (level)
  no operation moved by 1% of the time
where the time goes in v4:
time: 74.4 us; the launch traced here: 74.3 us
  Pallas kernels  73.7 us (99%)
    pallas_call x1, Pallas kernels, per_device(): pl.pallas_call(kernel, out_shape=jax.ShapeDtypeStruct((rows // nz, block_...  73.7 us

profile of v4, /device:TPU:1, one launch (start us, length us, event | category | flops | bytes accessed | tf_op | source)
XLA Modules:
  0.0 74.3 jit_solution(3749445213716817426)
XLA Ops:
  0.0 73.7 %shard_map.37 = f32[64,128]{1,0:T(8,128)S(1)} custom-call(bf16[8,2,4,16,512]{4,3,2,1,0:T(8,128)(2,1)} %bitcast.2, bf16[5,512,128]{2,1,0:T(8,128)(2,1)} %bitcast.3, s32[4,5]{1,0:T(4,128)} %band_mask.1), custom_call_target="tpu_custom_call" | custom-call | tf_op jit(solution)/shard_map/pallas_call | solution.py:412
  73.7 0.6 copy.5
